TPU v7x, 32 devices: a whole 2x2x4 slice. The times are simulated.
32 devices in a mesh: cand: 4 (over x, core), seq: 8 (over z, y).
Axes of the slice: x: 2, y: 2, z: 4, core: 2. Of those that a mesh axis runs over, the one named last changes fastest.
Arguments:
- response_query_array: bfloat16 [8, 768, 2560], P('cand', 'seq'), may hold values from -180 to 180
- response_key_array: bfloat16 [8, 768, 512], P('cand', 'seq'), may hold values from -6 to 6
- response_value_array: bfloat16 [8, 768, 512], P('cand', 'seq'), may hold values from -6 to 6
- prompt_key_array: bfloat16 [2048, 512], P(('cand', 'seq')), may hold values from -6 to 6
- prompt_value_array: bfloat16 [2048, 512], P(('cand', 'seq')), may hold values from -6 to 6
- lengths: int32 [8], replicated, may hold values from 192 to 768, as said below
- offsets: int32 [8], replicated, may hold values from 512 to 2048, as said below
- ranks: int32 [8], replicated, may hold values from 0 to 7, each once
Outputs:
- attention: bfloat16 [8, 768, 2560], P('cand', 'seq')
Inputs may be any that keep to these rules, and one draw needn't show every extreme that they name: `lengths`: some candidate's response has all 768 positions live. `offsets`: some candidate sees the whole prompt.
All inputs are finite; a program needn't handle non-finite values.
Results may differ from a plain program's by a relative error of at most 0.004.
Values may be sent and summed in bfloat16 or wider, within the bound.
No kernel may reach another device: no remote copies, remote signals or barrier semaphores. Data moves between devices by JAX's collectives and lax.ppermute only.
A program may use at most 128 MiB of HBM per device.

v0:
```python
import math
import jax
import jax.numpy as jnp
from jax import lax
from jax.sharding import PartitionSpec as P

QUERY_HEADS = 20
KEY_VALUE_HEADS = 4
HEAD_DIMENSION = 128
lowest_score_value = -1e30


def attend_block(running, query_rows, block_keys, block_values, allowed, shared):
    running_max, running_total, running_sum = running
    cand_count = query_rows.shape[0]
    heads_kv = query_rows.shape[2]
    head_size = query_rows.shape[4]
    score_scale = 1.0 / math.sqrt(head_size)
    if shared:
        keys_split = block_keys.reshape(block_keys.shape[0], heads_kv, head_size)
        values_split = block_values.reshape(block_values.shape[0], heads_kv, head_size)
        scores = jnp.einsum(
            "crhgd,nhd->chgrn", query_rows, keys_split, preferred_element_type=jnp.float32
        )
    else:
        keys_split = block_keys.reshape(cand_count, block_keys.shape[1], heads_kv, head_size)
        values_split = block_values.reshape(cand_count, block_values.shape[1], heads_kv, head_size)
        scores = jnp.einsum(
            "crhgd,cnhd->chgrn", query_rows, keys_split, preferred_element_type=jnp.float32
        )
    scores = jnp.where(allowed[:, None, None, :, :], scores * score_scale, -jnp.inf)
    new_max = jnp.maximum(running_max, jnp.max(scores, axis=-1))
    rescale = jnp.exp(running_max - new_max)
    exponent = jnp.exp(scores - new_max[..., None])
    weights = exponent.astype(jnp.bfloat16)
    new_total = running_total * rescale + jnp.sum(exponent, axis=-1)
    if shared:
        contrib = jnp.einsum(
            "chgrn,nhd->chgrd", weights, values_split, preferred_element_type=jnp.float32
        )
    else:
        contrib = jnp.einsum(
            "chgrn,cnhd->chgrd", weights, values_split, preferred_element_type=jnp.float32
        )
    new_sum = running_sum * rescale[..., None] + contrib
    return (new_max, new_total, new_sum)


def fold_blocks(
    running, query_rows, all_keys, all_values, key_pos, allowed_of, shared, live_of=None
):
    key_count = key_pos.shape[0]
    block_len = math.gcd(key_count, 512)
    keys_axis = 0 if shared else 1

    def one_block(step_at, carried):
        block_start = step_at * block_len
        block_keys = lax.dynamic_slice_in_dim(all_keys, block_start, block_len, keys_axis)
        block_values = lax.dynamic_slice_in_dim(all_values, block_start, block_len, keys_axis)
        block_pos = lax.dynamic_slice_in_dim(key_pos, block_start, block_len, 0)
        return attend_block(
            carried, query_rows, block_keys, block_values, allowed_of(block_pos), shared
        )

    return lax.fori_loop(0, key_count // block_len, one_block, running)


def body(
    response_query_array,
    response_key_array,
    response_value_array,
    prompt_key_array,
    prompt_value_array,
    lengths,
    offsets,
    ranks,
):
    candidate_local, output_rows, width = response_query_array.shape
    group_width = QUERY_HEADS // KEY_VALUE_HEADS
    group_at = lax.axis_index("cand")
    seq_at = lax.axis_index("seq")
    first_cand = group_at * candidate_local
    my_lengths = lax.dynamic_slice_in_dim(lengths, first_cand, candidate_local)
    my_offsets = lax.dynamic_slice_in_dim(offsets, first_cand, candidate_local)
    query_pos = seq_at * output_rows + jnp.arange(output_rows, dtype=jnp.int32)
    query_rows = response_query_array.reshape(
        candidate_local, output_rows, KEY_VALUE_HEADS, group_width, HEAD_DIMENSION
    )
    pieces = (
        lax.all_gather(prompt_key_array, ("cand", "seq"), axis=0, tiled=True),
        lax.all_gather(prompt_value_array, ("cand", "seq"), axis=0, tiled=True),
    )
    key_pos = jnp.arange(pieces[0].shape[0], dtype=jnp.int32)

    def allowed_of(block_pos):
        return block_pos[None, None, :] < my_offsets[:, None, None]

    running = fold_blocks(
        (
            jnp.full(
                (candidate_local, KEY_VALUE_HEADS, group_width, output_rows),
                lowest_score_value,
                jnp.float32,
            ),
            jnp.zeros((candidate_local, KEY_VALUE_HEADS, group_width, output_rows), jnp.float32),
            jnp.zeros(
                (candidate_local, KEY_VALUE_HEADS, group_width, output_rows, HEAD_DIMENSION),
                jnp.float32,
            ),
        ),
        query_rows,
        pieces[0],
        pieces[1],
        key_pos,
        allowed_of,
        True,
    )
    pieces = (
        lax.all_gather(response_key_array, "seq", axis=1, tiled=True),
        lax.all_gather(response_value_array, "seq", axis=1, tiled=True),
    )
    key_pos = jnp.arange(pieces[0].shape[1], dtype=jnp.int32)

    def allowed_of(block_pos):
        causal = block_pos[None, None, :] <= query_pos[None, :, None]
        return causal & (block_pos[None, None, :] < my_lengths[:, None, None])

    final_max, final_total, final_sum = fold_blocks(
        running, query_rows, pieces[0], pieces[1], key_pos, allowed_of, False
    )
    attended = final_sum / final_total[..., None]
    attended = jnp.transpose(attended, (0, 3, 1, 2, 4)).reshape(candidate_local, output_rows, width)
    row_valid = query_pos[None, :] < my_lengths[:, None]
    attended = jnp.where(row_valid[:, :, None], attended, 0.0).astype(jnp.bfloat16)
    gathered = lax.all_gather(attended, "cand", axis=0, tiled=True)
    every_cand = jnp.arange(gathered.shape[0], dtype=jnp.int32)
    chosen = []
    for within in range(candidate_local):
        target = first_cand + within
        source = jnp.sum(jnp.where(ranks == target, every_cand, 0))
        chosen.append(lax.dynamic_index_in_dim(gathered, source, 0, keepdims=False))
    return jnp.stack(chosen, axis=0)


def solution(mesh):
    in_specs = (
        P("cand", "seq", None),
        P("cand", "seq", None),
        P("cand", "seq", None),
        P(("cand", "seq"), None),
        P(("cand", "seq"), None),
        P(),
        P(),
        P(),
    )
    out_specs = P("cand", "seq", None)
    return jax.shard_map(body, mesh=mesh, in_specs=in_specs, out_specs=out_specs, check_vma=False)
```

profile of v0, /device:TPU:0, one launch (start us, length us, event | category | flops | bytes accessed | tf_op | source)
XLA Modules:
  0.0 304.9 jit_solution(10088347945177968936)
XLA Ops:
  6.5 0.7 all-gather.6.cloned.1.call-update
  8.1 1.8 copy.56
  9.9 1.8 copy.57
  11.9 1.7 copy.52
  14.3 1.4 copy.62
  15.9 53.7 %all-gather.6.cloned.1.call-done = bf16[2048,512]{1,0:T(8,128)(2,1)} async-done(((bf16[64,512]{1,0:T(8,128)(2,1)}), bf16[2048,512]{1,0:T(8,128)(2,1)}) %all-gather.6.cloned.1.call-update) | async-done | bytes 2097168 | tf_op jit(solution)/shard_map/all_gather | solution.py:90
  69.6 58.4 %all-gather.8.cloned.1.call-done = bf16[2048,512]{1,0:T(8,128)(2,1)} async-done(((bf16[64,512]{1,0:T(8,128)(2,1)}), bf16[2048,512]{1,0:T(8,128)(2,1)}) %all-gather.8.cloned.1.call-update) | async-done | bytes 2097168 | tf_op jit(solution)/shard_map/all_gather | solution.py:91
  128.0 65.4 %while.37 = (s32[]{:T(128)}, f32[2,4,5,96]{3,2,0,1:T(8,128)S(1)}, f32[2,4,5,96]{3,2,0,1:T(8,128)S(1)}, f32[2,4,5,96,128]{4,3,2,0,1:T(8,128)}, s32[2048]{0:T(1024...) while((s32[]{:T(128)}, f32[2,4,5,96]{3,2,0,1:T(8,128)S(1)}, ...), condition=%wide.region_3.4_spmd.clone, body=%wide.region_0.3_spmd.clone.sunk | while | flops 1029754624 | bytes 34007236 | solution.py:65
  128.1 1.3 constant_dynamic-slice_fusion.9
  129.6 4.2 %fusion.60 = (f32[2,4,5,96]{3,2,0,1:T(8,128)S(1)}, f32[4,512,2,96,5]{1,3,4,2,0:T(8,128)}) fusion(pred[2,512]{1,0:T(4,128)(4,1)S(1)} %broadcast_compare_fusion.9, bf16[512,4,128,1,1]{0,2,4,3,1:T(8,128)(2,1)S(1)} %bitcast.88, bf16[2,96,4,5,128]{4,1,3,0,2:T(8,128)(2,1)S(1)} %get-tuple-element.683), kind=kOutput, calls=%fused_computation.26.clone.1 | convolution fusion | flops 509210880 | bytes 9388032 | tf_op jit(solution)/shard_map/while/body/eval_jaxpr/crhgd,nhd->chgrn/dot_general | solution.py:22
  133.9 4.5 %fusion.61 = f32[2,4,5,96]{3,2,0,1:T(8,128)S(1)} fusion(f32[4,512,2,96,5]{1,3,4,2,0:T(8,128)} %get-tuple-element.646, f32[2,4,5,96]{3,2,0,1:T(8,128)S(1)} %select_maximum_fusion.2, pred[2,512]{1,0:T(4,128)(4,1)S(1)} %broadcast_compare_fusion.9), kind=kLoop, calls=%fused_computation.25.clone.1 | loop fusion | flops 7860480 | bytes 7896064 | tf_op jit(solution)/shard_map/while/body/eval_jaxpr/reduce_sum | solution.py:36
  138.6 5.4 %bitcast_add_fusion.2 = f32[2,4,5,96,128]{4,3,2,0,1:T(8,128)} fusion(f32[2,4,5,96,128]{4,3,2,0,1:T(8,128)} %get-tuple-element.666, bf16[512,4,128,1,1]{0,2,4,3,1:T(8,128)(2,1)S(1)} %bitcast.91, f32[4,512,2,96,5]{1,3,4,2,0:T(8,128)} %get-tuple-element.646, f32[2,4,5,96]{3,2,0,1:T(8,128)S(1)} %select_maximum_fusion.2, ...), kind=kOutput, calls=%fused_computation.32.clone.1 | convolution fusion | flops 512655360 | bytes 12352513 | tf_op jit(solution)/shard_map/while/body/eval_jaxpr/chgrn,nhd->chgrd/dot_general | solution.py:38
  144.2 1.3 constant_dynamic-slice_fusion.9
  145.7 4.2 %fusion.60 = (f32[2,4,5,96]{3,2,0,1:T(8,128)S(1)}, f32[4,512,2,96,5]{1,3,4,2,0:T(8,128)}) fusion(pred[2,512]{1,0:T(4,128)(4,1)S(1)} %broadcast_compare_fusion.9, bf16[512,4,128,1,1]{0,2,4,3,1:T(8,128)(2,1)S(1)} %bitcast.88, bf16[2,96,4,5,128]{4,1,3,0,2:T(8,128)(2,1)S(1)} %get-tuple-element.683), kind=kOutput, calls=%fused_computation.26.clone.1 | convolution fusion | flops 509210880 | bytes 9388032 | tf_op jit(solution)/shard_map/while/body/eval_jaxpr/crhgd,nhd->chgrn/dot_general | solution.py:22
  149.9 4.4 %fusion.61 = f32[2,4,5,96]{3,2,0,1:T(8,128)S(1)} fusion(f32[4,512,2,96,5]{1,3,4,2,0:T(8,128)} %get-tuple-element.646, f32[2,4,5,96]{3,2,0,1:T(8,128)S(1)} %select_maximum_fusion.2, pred[2,512]{1,0:T(4,128)(4,1)S(1)} %broadcast_compare_fusion.9), kind=kLoop, calls=%fused_computation.25.clone.1 | loop fusion | flops 7860480 | bytes 7896064 | tf_op jit(solution)/shard_map/while/body/eval_jaxpr/reduce_sum | solution.py:36
  154.6 6.0 %bitcast_add_fusion.2 = f32[2,4,5,96,128]{4,3,2,0,1:T(8,128)} fusion(f32[2,4,5,96,128]{4,3,2,0,1:T(8,128)} %get-tuple-element.666, bf16[512,4,128,1,1]{0,2,4,3,1:T(8,128)(2,1)S(1)} %bitcast.91, f32[4,512,2,96,5]{1,3,4,2,0:T(8,128)} %get-tuple-element.646, f32[2,4,5,96]{3,2,0,1:T(8,128)S(1)} %select_maximum_fusion.2, ...), kind=kOutput, calls=%fused_computation.32.clone.1 | convolution fusion | flops 512655360 | bytes 12352513 | tf_op jit(solution)/shard_map/while/body/eval_jaxpr/chgrn,nhd->chgrd/dot_general | solution.py:38
  160.7 1.3 constant_dynamic-slice_fusion.9
  162.2 4.2 %fusion.60 = (f32[2,4,5,96]{3,2,0,1:T(8,128)S(1)}, f32[4,512,2,96,5]{1,3,4,2,0:T(8,128)}) fusion(pred[2,512]{1,0:T(4,128)(4,1)S(1)} %broadcast_compare_fusion.9, bf16[512,4,128,1,1]{0,2,4,3,1:T(8,128)(2,1)S(1)} %bitcast.88, bf16[2,96,4,5,128]{4,1,3,0,2:T(8,128)(2,1)S(1)} %get-tuple-element.683), kind=kOutput, calls=%fused_computation.26.clone.1 | convolution fusion | flops 509210880 | bytes 9388032 | tf_op jit(solution)/shard_map/while/body/eval_jaxpr/crhgd,nhd->chgrn/dot_general | solution.py:22
  166.4 4.4 %fusion.61 = f32[2,4,5,96]{3,2,0,1:T(8,128)S(1)} fusion(f32[4,512,2,96,5]{1,3,4,2,0:T(8,128)} %get-tuple-element.646, f32[2,4,5,96]{3,2,0,1:T(8,128)S(1)} %select_maximum_fusion.2, pred[2,512]{1,0:T(4,128)(4,1)S(1)} %broadcast_compare_fusion.9), kind=kLoop, calls=%fused_computation.25.clone.1 | loop fusion | flops 7860480 | bytes 7896064 | tf_op jit(solution)/shard_map/while/body/eval_jaxpr/reduce_sum | solution.py:36
  171.1 5.9 %bitcast_add_fusion.2 = f32[2,4,5,96,128]{4,3,2,0,1:T(8,128)} fusion(f32[2,4,5,96,128]{4,3,2,0,1:T(8,128)} %get-tuple-element.666, bf16[512,4,128,1,1]{0,2,4,3,1:T(8,128)(2,1)S(1)} %bitcast.91, f32[4,512,2,96,5]{1,3,4,2,0:T(8,128)} %get-tuple-element.646, f32[2,4,5,96]{3,2,0,1:T(8,128)S(1)} %select_maximum_fusion.2, ...), kind=kOutput, calls=%fused_computation.32.clone.1 | convolution fusion | flops 512655360 | bytes 12352513 | tf_op jit(solution)/shard_map/while/body/eval_jaxpr/chgrn,nhd->chgrd/dot_general | solution.py:38
  177.1 1.3 constant_dynamic-slice_fusion.9
  178.6 4.2 %fusion.60 = (f32[2,4,5,96]{3,2,0,1:T(8,128)S(1)}, f32[4,512,2,96,5]{1,3,4,2,0:T(8,128)}) fusion(pred[2,512]{1,0:T(4,128)(4,1)S(1)} %broadcast_compare_fusion.9, bf16[512,4,128,1,1]{0,2,4,3,1:T(8,128)(2,1)S(1)} %bitcast.88, bf16[2,96,4,5,128]{4,1,3,0,2:T(8,128)(2,1)S(1)} %get-tuple-element.683), kind=kOutput, calls=%fused_computation.26.clone.1 | convolution fusion | flops 509210880 | bytes 9388032 | tf_op jit(solution)/shard_map/while/body/eval_jaxpr/crhgd,nhd->chgrn/dot_general | solution.py:22
  182.8 4.4 %fusion.61 = f32[2,4,5,96]{3,2,0,1:T(8,128)S(1)} fusion(f32[4,512,2,96,5]{1,3,4,2,0:T(8,128)} %get-tuple-element.646, f32[2,4,5,96]{3,2,0,1:T(8,128)S(1)} %select_maximum_fusion.2, pred[2,512]{1,0:T(4,128)(4,1)S(1)} %broadcast_compare_fusion.9), kind=kLoop, calls=%fused_computation.25.clone.1 | loop fusion | flops 7860480 | bytes 7896064 | tf_op jit(solution)/shard_map/while/body/eval_jaxpr/reduce_sum | solution.py:36
  187.5 5.9 %bitcast_add_fusion.2 = f32[2,4,5,96,128]{4,3,2,0,1:T(8,128)} fusion(f32[2,4,5,96,128]{4,3,2,0,1:T(8,128)} %get-tuple-element.666, bf16[512,4,128,1,1]{0,2,4,3,1:T(8,128)(2,1)S(1)} %bitcast.91, f32[4,512,2,96,5]{1,3,4,2,0:T(8,128)} %get-tuple-element.646, f32[2,4,5,96]{3,2,0,1:T(8,128)S(1)} %select_maximum_fusion.2, ...), kind=kOutput, calls=%fused_computation.32.clone.1 | convolution fusion | flops 512655360 | bytes 12352513 | tf_op jit(solution)/shard_map/while/body/eval_jaxpr/chgrn,nhd->chgrd/dot_general | solution.py:38
  193.4 1.7 copy.60
  196.3 22.1 %all-gather.12.cloned.1.call-done = bf16[2,768,512]{2,0,1:T(2,128)(2,1)} async-done(((bf16[2,96,512]{2,0,1:T(2,128)(2,1)}), bf16[2,768,512]{2,0,1:T(2,128)(2,1)}) %all-gather.12.cloned.1.call-update) | async-done | bytes 1572880 | tf_op jit(solution)/shard_map/all_gather | solution.py:120
  218.4 41.8 %while.36 = (s32[]{:T(128)}, f32[2,4,5,96]{3,2,1,0:T(8,128)}, f32[2,4,5,96]{3,2,1,0:T(8,128)}, f32[2,4,5,96,128]{4,3,2,1,0:T(8,128)S(1)}, s32[768]{0:T(1024)S(1)...) while((s32[]{:T(128)}, f32[2,4,5,96]{3,2,1,0:T(8,128)}, ...), condition=%wide.region_7.8_spmd.clone, body=%wide.region_4.7_spmd.clone.sunk | while | flops 515194976 | bytes 38561872 | solution.py:65
  219.3 1.9 constant_dynamic-slice_fusion.8
  221.8 2.2 fusion.54
  224.0 1.8 copy-done
  225.9 1.5 fusion.55
  228.0 3.7 %multiply_add_fusion.5 = f32[2,4,5,96,128]{4,3,2,1,0:T(8,128)S(1)} fusion(f32[2,4,5,96,128]{4,3,2,1,0:T(8,128)S(1)} %get-tuple-element.706, bf16[2,256,4,128,1]{1,3,4,2,0:T(8,128)(2,1)S(1)} %bitcast.89, f32[2,4,256,96,5]{2,3,4,1,0:T(8,128)} %copy-done, f32[2,4,5,96]{3,2,1,0:T(8,128)S(1)} %max.19, pred[2,96,256]{2,1,0:T(8,128)(4,1)S(1)} %copy-done.1, ...), kind=kOutput, calls=%fused_computation.7.clone.1 | convolution fusion | flops 256573440 | bytes 8468480 | tf_op jit(solution)/shard_map/while/body/eval_jaxpr/chgrn,cnhd->chgrd/dot_general | solution.py:42
  233.2 1.9 constant_dynamic-slice_fusion.8
  235.7 2.2 fusion.54
  238.0 1.8 copy-done
  239.8 1.5 fusion.55
  241.9 3.7 %multiply_add_fusion.5 = f32[2,4,5,96,128]{4,3,2,1,0:T(8,128)S(1)} fusion(f32[2,4,5,96,128]{4,3,2,1,0:T(8,128)S(1)} %get-tuple-element.706, bf16[2,256,4,128,1]{1,3,4,2,0:T(8,128)(2,1)S(1)} %bitcast.89, f32[2,4,256,96,5]{2,3,4,1,0:T(8,128)} %copy-done, f32[2,4,5,96]{3,2,1,0:T(8,128)S(1)} %max.19, pred[2,96,256]{2,1,0:T(8,128)(4,1)S(1)} %copy-done.1, ...), kind=kOutput, calls=%fused_computation.7.clone.1 | convolution fusion | flops 256573440 | bytes 8468480 | tf_op jit(solution)/shard_map/while/body/eval_jaxpr/chgrn,cnhd->chgrd/dot_general | solution.py:42
  247.2 1.9 constant_dynamic-slice_fusion.8
  249.7 2.2 fusion.54
  251.9 1.8 copy-done
  253.7 1.5 fusion.55
  255.9 3.7 %multiply_add_fusion.5 = f32[2,4,5,96,128]{4,3,2,1,0:T(8,128)S(1)} fusion(f32[2,4,5,96,128]{4,3,2,1,0:T(8,128)S(1)} %get-tuple-element.706, bf16[2,256,4,128,1]{1,3,4,2,0:T(8,128)(2,1)S(1)} %bitcast.89, f32[2,4,256,96,5]{2,3,4,1,0:T(8,128)} %copy-done, f32[2,4,5,96]{3,2,1,0:T(8,128)S(1)} %max.19, pred[2,96,256]{2,1,0:T(8,128)(4,1)S(1)} %copy-done.1, ...), kind=kOutput, calls=%fused_computation.7.clone.1 | convolution fusion | flops 256573440 | bytes 8468480 | tf_op jit(solution)/shard_map/while/body/eval_jaxpr/chgrn,cnhd->chgrd/dot_general | solution.py:42
  260.2 1.3 divide_bitcast_fusion
  261.5 0.8 copy.64
  262.9 1.2 select_convert_fusion
  268.5 27.6 %all-gather.14.cloned.1.call-done = bf16[8,96,2560]{2,1,0:T(8,128)(2,1)} async-done(((bf16[2,96,2560]{2,1,0:T(8,128)(2,1)}), bf16[8,96,2560]{2,1,0:T(8,128)(2,1)}) %all-gather.14.cloned.1.call-update) | async-done | bytes 3932176 | tf_op jit(solution)/shard_map/all_gather | solution.py:135
  296.1 1.2 constant_dynamic-slice_fusion.5
  297.3 1.0 pad_maximum_fusion
  (115 shorter events, 14.7 us)
Async XLA Ops:
  6.5 63.1 %all-gather.6.cloned.1.call-start = ((), (), s32[]{:S(2)}) async-start(), calls=%async_computation | async-start | bytes 2162688 | tf_op jit(solution)/shard_map/all_gather | solution.py:90
  7.3 120.7 %all-gather.8.cloned.1.call-start = ((), (), s32[]{:S(2)}) async-start(), calls=%async_computation.1 | async-start | bytes 2162688 | tf_op jit(solution)/shard_map/all_gather | solution.py:91
  8.0 188.3 %all-gather.10.cloned.1.call-start = ((), (), s32[]{:S(2)}) async-start(), calls=%async_computation.2 | async-start | bytes 1769472 | tf_op jit(solution)/shard_map/all_gather | solution.py:119
  9.9 5.8 %copy-start.6 = (s32[8]{0:T(128)S(1)}, s32[8]{0:T(128)}, u32[]{:S(2)}) copy-start(s32[8]{0:T(128)} %param.18) | copy-start | bytes 100
  9.9 5.9 %copy-start.7 = (s32[8]{0:T(128)S(1)}, s32[8]{0:T(128)}, u32[]{:S(2)}) copy-start(s32[8]{0:T(128)} %param.17) | copy-start | bytes 100
  9.9 208.5 %all-gather.12.cloned.1.call-start = ((), (), s32[]{:S(2)}) async-start(), calls=%async_computation.3 | async-start | bytes 1769472 | tf_op jit(solution)/shard_map/all_gather | solution.py:120
  11.8 284.3 %all-gather.14.cloned.1.call-start = ((), (), s32[]{:S(2)}) async-start(), calls=%async_computation.4 | async-start | bytes 4915200 | tf_op jit(solution)/shard_map/all_gather | solution.py:135
  221.8 2.2 copy-start.2
  221.8 4.1 %copy-start.1 = (pred[2,96,256]{2,1,0:T(8,128)(4,1)S(1)}, pred[2,96,256]{2,1,0:T(8,128)(4,1)}, u32[]{:S(2)}) copy-start(pred[2,96,256]{2,1,0:T(8,128)(4,1)} %broadcast_and_fusion.2) | copy-start | bytes 147460 | tf_op jit(solution)/shard_map/while
  221.8 5.6 %copy-start.3 = (f32[2,4,5,96]{3,2,1,0:T(8,128)S(1)}, f32[2,4,5,96]{3,2,1,0:T(8,128)}, u32[]{:S(2)}) copy-start(f32[2,4,5,96]{3,2,1,0:T(8,128)} %get-tuple-element.705) | copy-start | bytes 46084 | tf_op jit(solution)/shard_map/while
  224.0 1.8 copy-start
  227.4 4.3 %copy-start.4 = (f32[2,4,5,96]{3,2,1,0:T(8,128)}, f32[2,4,5,96]{3,2,1,0:T(8,128)S(1)}, u32[]{:S(2)}) copy-start(f32[2,4,5,96]{3,2,1,0:T(8,128)S(1)} %get-tuple-element.719) | copy-start | bytes 46084 | tf_op jit(solution)/shard_map/while
  235.7 2.2 copy-start.2
  235.7 4.1 %copy-start.1 = (pred[2,96,256]{2,1,0:T(8,128)(4,1)S(1)}, pred[2,96,256]{2,1,0:T(8,128)(4,1)}, u32[]{:S(2)}) copy-start(pred[2,96,256]{2,1,0:T(8,128)(4,1)} %broadcast_and_fusion.2) | copy-start | bytes 147460 | tf_op jit(solution)/shard_map/while
  235.7 5.6 %copy-start.3 = (f32[2,4,5,96]{3,2,1,0:T(8,128)S(1)}, f32[2,4,5,96]{3,2,1,0:T(8,128)}, u32[]{:S(2)}) copy-start(f32[2,4,5,96]{3,2,1,0:T(8,128)} %get-tuple-element.705) | copy-start | bytes 46084 | tf_op jit(solution)/shard_map/while
  237.9 1.8 copy-start
  241.4 4.3 %copy-start.4 = (f32[2,4,5,96]{3,2,1,0:T(8,128)}, f32[2,4,5,96]{3,2,1,0:T(8,128)S(1)}, u32[]{:S(2)}) copy-start(f32[2,4,5,96]{3,2,1,0:T(8,128)S(1)} %get-tuple-element.719) | copy-start | bytes 46084 | tf_op jit(solution)/shard_map/while
  249.6 2.2 copy-start.2
  249.6 4.1 %copy-start.1 = (pred[2,96,256]{2,1,0:T(8,128)(4,1)S(1)}, pred[2,96,256]{2,1,0:T(8,128)(4,1)}, u32[]{:S(2)}) copy-start(pred[2,96,256]{2,1,0:T(8,128)(4,1)} %broadcast_and_fusion.2) | copy-start | bytes 147460 | tf_op jit(solution)/shard_map/while
  249.7 5.6 %copy-start.3 = (f32[2,4,5,96]{3,2,1,0:T(8,128)S(1)}, f32[2,4,5,96]{3,2,1,0:T(8,128)}, u32[]{:S(2)}) copy-start(f32[2,4,5,96]{3,2,1,0:T(8,128)} %get-tuple-element.705) | copy-start | bytes 46084 | tf_op jit(solution)/shard_map/while
  251.9 1.8 copy-start
  255.3 4.3 %copy-start.4 = (f32[2,4,5,96]{3,2,1,0:T(8,128)}, f32[2,4,5,96]{3,2,1,0:T(8,128)S(1)}, u32[]{:S(2)}) copy-start(f32[2,4,5,96]{3,2,1,0:T(8,128)S(1)} %get-tuple-element.719) | copy-start | bytes 46084 | tf_op jit(solution)/shard_map/while
  261.5 2.6 copy-start.5
Sparse Core Ops, SparseCore 0:
  10.3 59.2 all-gather.5
  72.6 55.3 all-gather.7
  130.2 43.0 all-gather.9
  175.3 43.0 all-gather.11
  264.3 31.7 all-gather.13
where the time goes:
time: 306 us; the launch traced here: 305 us
  waiting for transfers between devices  163 us (53%)
  matrix products  57.7 us (19%)
  local copies, waits for them, and re-layouts  36.7 us (12%)
  other arithmetic  29.6 us (10%)
  between operations  16.9 us (6%)
    all_gather x1, waiting for transfers between devices, body(): lax.all_gather(prompt_value_array, ('cand', 'seq'), axis=0, tiled=True)  58.4 us
    all_gather x1, waiting for transfers between devices, body(): lax.all_gather(prompt_key_array, ('cand', 'seq'), axis=0, tiled=True)  53.7 us
    all_gather x1, waiting for transfers between devices, body(): gathered = lax.all_gather(attended, 'cand', axis=0, tiled=True)  27.6 us
    dot_general x4, matrix products, attend_block(): jnp.einsum('chgrn,nhd->chgrd', weights, values_split, preferred_element_t...  23.1 us
    reduce_sum x7, other arithmetic, attend_block(): new_total = running_total * rescale + jnp.sum(exponent, axis=-1)  22.3 us
    all_gather x1, waiting for transfers between devices, body(): lax.all_gather(response_value_array, 'seq', axis=1, tiled=True)  22.1 us
    dot_general x4, matrix products, attend_block(): jnp.einsum('crhgd,nhd->chgrn', query_rows, keys_split, preferred_element_...  16.9 us
    dynamic_slice x14, local copies, waits for them, and re-layouts, one_block(): lax.dynamic_slice_in_dim(all_values, block_start, block_len, keys_axis)  13.3 us
  transfers between devices with their start and end apart: 5, of which 4 were waited for; matrix products, arithmetic and copies ran while one was open for 25% of the time, Pallas kernels for 0%

commit v1 on v0

--- a/solution.py
+++ b/solution.py
@@ -132,7 +132,12 @@
     attended = jnp.transpose(attended, (0, 3, 1, 2, 4)).reshape(candidate_local, output_rows, width)
     row_valid = query_pos[None, :] < my_lengths[:, None]
     attended = jnp.where(row_valid[:, :, None], attended, 0.0).astype(jnp.bfloat16)
-    gathered = lax.all_gather(attended, "cand", axis=0, tiled=True)
+    ring = [attended]
+    for hop in range(3):
+        ring.append(lax.ppermute(ring[-1], "cand", [(dev, (dev + 1) % 4) for dev in range(4)]))
+    gathered = jnp.roll(
+        jnp.concatenate(ring[::-1], axis=0), (lax.axis_index("cand") + 1) * ring[0].shape[0], axis=0
+    )
     every_cand = jnp.arange(gathered.shape[0], dtype=jnp.int32)
     chosen = []
     for within in range(candidate_local):

time: 306 us -> 313 us (1.023)
  waiting for transfers between devices: 163 us -> 197 us
  matrix products: 57.7 us -> 27 us
  local copies, waits for them, and re-layouts: 36.7 us -> 49.8 us
  other arithmetic: 29.6 us -> 20.2 us
    ppermute x0 -> x3, waiting for transfers between devices: none -> 32.4 us  [body(): lax.ppermute(ring[-1], 'cand', [(dev, (dev + 1) % 4) for dev in range(4)])]
    all_gather x1 -> x0, waiting for transfers between devices: 27.6 us -> none  [body(): gathered = lax.all_gather(attended, 'cand', axis=0, tiled=True)]
    all_gather x1, waiting for transfers between devices: 22.1 us -> 45.1 us  [body(): lax.all_gather(response_value_array, 'seq', axis=1, tiled=True)]
    dot_general x4, matrix products: 23.1 us -> 9.53 us  [attend_block(): jnp.einsum('chgrn,nhd->chgrd', weights, values_split, preferred_element_t...]
    dot_general x4, matrix products: 16.9 us -> 5.01 us  [attend_block(): jnp.einsum('crhgd,nhd->chgrn', query_rows, keys_split, preferred_element_...]
    reduce_sum x7, other arithmetic: 22.3 us -> 13.5 us  [attend_block(): new_total = running_total * rescale + jnp.sum(exponent, axis=-1)]
    ppermute x0 -> x3, local copies, waits for them, and re-layouts: none -> 6.47 us  [body(): lax.ppermute(ring[-1], 'cand', [(dev, (dev + 1) % 4) for dev in range(4)])]
    all_gather x1, waiting for transfers between devices: 0.01 us -> 5.95 us  [body(): lax.all_gather(response_key_array, 'seq', axis=1, tiled=True)]
  transfers between devices with their start and end apart: 5 -> 7, of which waited for: 4 -> 7; matrix products, arithmetic and copies ran while one was open for 25% -> 15% of each run, Pallas kernels for 0% -> 0%
where the time goes in v1:
time: 313 us; the launch traced here: 312 us
  waiting for transfers between devices  197 us (63%)
  local copies, waits for them, and re-layouts  49.8 us (16%)
  matrix products  27 us (9%)
  other arithmetic  20.2 us (6%)
  between operations  17.1 us (5%)
    all_gather x1, waiting for transfers between devices, body(): lax.all_gather(prompt_value_array, ('cand', 'seq'), axis=0, tiled=True)  58.4 us
    all_gather x1, waiting for transfers between devices, body(): lax.all_gather(prompt_key_array, ('cand', 'seq'), axis=0, tiled=True)  53.8 us
    all_gather x1, waiting for transfers between devices, body(): lax.all_gather(response_value_array, 'seq', axis=1, tiled=True)  45.1 us
    ppermute x3, waiting for transfers between devices, body(): lax.ppermute(ring[-1], 'cand', [(dev, (dev + 1) % 4) for dev in range(4)])  32.4 us
    unnamed x27, local copies, waits for them, and re-layouts  15.9 us
    reduce_sum x7, other arithmetic, attend_block(): new_total = running_total * rescale + jnp.sum(exponent, axis=-1)  13.5 us
    dynamic_slice x14, local copies, waits for them, and re-layouts, one_block(): lax.dynamic_slice_in_dim(all_values, block_start, block_len, keys_axis)  13.3 us
    dot_general x4, matrix products, attend_block(): jnp.einsum('chgrn,nhd->chgrd', weights, values_split, preferred_element_t...  9.53 us
  transfers between devices with their start and end apart: 7, of which 7 were waited for; matrix products, arithmetic and copies ran while one was open for 15% of the time, Pallas kernels for 0%

profile of v1, /device:TPU:0, one launch (start us, length us, event | category | flops | bytes accessed | tf_op | source)
XLA Modules:
  0.0 312.1 jit_solution(17494399664443600206)
XLA Ops:
  8.1 1.8 copy.38
  9.9 1.8 copy.39
  11.8 1.7 copy.34
  13.5 1.4 copy.44
  15.8 53.8 %all-gather.5.cloned.1.call-done = bf16[2048,512]{1,0:T(8,128)(2,1)} async-done(((bf16[64,512]{1,0:T(8,128)(2,1)}), bf16[2048,512]{1,0:T(8,128)(2,1)}) %all-gather.5.cloned.1.call-update) | async-done | bytes 2097168 | tf_op jit(solution)/shard_map/all_gather | solution.py:90
  69.6 58.4 %all-gather.7.cloned.1.call-done = bf16[2048,512]{1,0:T(8,128)(2,1)} async-done(((bf16[64,512]{1,0:T(8,128)(2,1)}), bf16[2048,512]{1,0:T(8,128)(2,1)}) %all-gather.7.cloned.1.call-update) | async-done | bytes 2097168 | tf_op jit(solution)/shard_map/all_gather | solution.py:91
  128.0 36.4 %while.37 = (s32[]{:T(128)}, f32[2,4,5,96]{3,2,0,1:T(8,128)S(1)}, f32[2,4,5,96]{3,2,0,1:T(8,128)S(1)}, f32[2,4,5,96,128]{4,3,2,0,1:T(8,128)}, s32[2048]{0:T(1024...) while((s32[]{:T(128)}, f32[2,4,5,96]{3,2,0,1:T(8,128)S(1)}, ...), condition=%wide.region_3.4_spmd.clone, body=%wide.region_0.3_spmd.clone.sunk | while | flops 1029754624 | bytes 49735940 | solution.py:65
  128.1 1.3 constant_dynamic-slice_fusion.9
  131.1 2.2 fusion.62
  133.4 2.4 bitcast_add_fusion.2
  137.2 1.3 constant_dynamic-slice_fusion.9
  140.2 2.2 fusion.62
  142.5 2.4 bitcast_add_fusion.2
  144.9 1.3 copy-done.5
  146.3 1.3 constant_dynamic-slice_fusion.9
  149.3 2.2 fusion.62
  151.6 2.4 bitcast_add_fusion.2
  155.4 1.3 constant_dynamic-slice_fusion.9
  158.4 2.2 fusion.62
  160.7 2.4 bitcast_add_fusion.2
  163.1 1.3 copy-done.5
  164.4 1.7 copy.42
  167.3 5.9 %all-gather.9.cloned.1.call-done = bf16[2,768,512]{2,0,1:T(2,128)(2,1)} async-done(((bf16[2,96,512]{2,0,1:T(2,128)(2,1)}), bf16[2,768,512]{2,0,1:T(2,128)(2,1)}) %all-gather.9.cloned.1.call-update) | async-done | bytes 1572880 | tf_op jit(solution)/shard_map/all_gather | solution.py:119
  173.3 45.1 %all-gather.11.cloned.1.call-done = bf16[2,768,512]{2,0,1:T(2,128)(2,1)} async-done(((bf16[2,96,512]{2,0,1:T(2,128)(2,1)}), bf16[2,768,512]{2,0,1:T(2,128)(2,1)}) %all-gather.11.cloned.1.call-update) | async-done | bytes 1572880 | tf_op jit(solution)/shard_map/all_gather | solution.py:120
  218.3 31.1 %while.36 = (s32[]{:T(128)}, f32[2,4,5,96]{3,2,1,0:T(8,128)}, f32[2,4,5,96]{3,2,1,0:T(8,128)}, f32[2,4,5,96,128]{4,3,2,1,0:T(8,128)S(1)}, s32[768]{0:T(1024)S(1)...) while((s32[]{:T(128)}, f32[2,4,5,96]{3,2,1,0:T(8,128)}, ...), condition=%wide.region_7.8_spmd.clone, body=%wide.region_4.7_spmd.clone.sunk | while | flops 515194976 | bytes 22833208 | solution.py:65
  219.2 1.9 constant_dynamic-slice_fusion.8
  222.3 2.2 fusion.55
  224.5 1.5 fusion.56
  226.1 2.0 multiply_add_fusion.5
  229.6 1.9 constant_dynamic-slice_fusion.8
  232.6 2.2 fusion.55
  234.9 1.5 fusion.56
  236.5 2.0 multiply_add_fusion.5
  240.0 1.9 constant_dynamic-slice_fusion.8
  243.0 2.2 fusion.55
  245.3 1.5 fusion.56
  246.9 2.0 multiply_add_fusion.5
  249.4 2.3 divide_bitcast_fusion
  251.7 1.7 copy.46
  254.7 13.5 %collective-permute-done = bf16[2,96,2560]{2,1,0:T(8,128)(2,1)S(1)} collective-permute-done((bf16[2,96,2560]{2,1,0:T(8,128)(2,1)S(1)}, bf16[2,96,2560]{2,1,0:T(8,128)(2,1)S(1)}, u32[]{:S(2)}, u32[]{:S(2)}) %collective-permute-start) | collective-permute-done | bytes 983072 | tf_op jit(solution)/shard_map/ppermute | solution.py:137
  269.1 13.6 %collective-permute-done.1 = bf16[2,96,2560]{2,1,0:T(8,128)(2,1)} collective-permute-done((bf16[2,96,2560]{2,1,0:T(8,128)(2,1)S(1)}, bf16[2,96,2560]{2,1,0:T(8,128)(2,1)}, u32[]{:S(2)}, u32[]{:S(2)}) %collective-permute-start.1) | collective-permute-done | bytes 983072 | tf_op jit(solution)/shard_map/ppermute | solution.py:137
  287.2 1.7 copy.50
  288.9 2.4 copy.49
  291.3 5.2 %collective-permute-done.2 = bf16[2,96,2560]{2,1,0:T(8,128)(2,1)} collective-permute-done((bf16[2,96,2560]{2,1,0:T(8,128)(2,1)}, bf16[2,96,2560]{2,1,0:T(8,128)(2,1)}, u32[]{:S(2)}, u32[]{:S(2)}) %collective-permute-start.2) | collective-permute-done | bytes 983072 | tf_op jit(solution)/shard_map/ppermute | solution.py:137
  296.6 2.4 copy.48
  299.0 1.4 constant_dynamic-update-slice_fusion.7
  300.4 1.6 constant_dynamic-update-slice_fusion.6
  304.2 1.4 copy.54
  (146 shorter events, 26.6 us)
Async XLA Ops:
  6.5 63.1 %all-gather.5.cloned.1.call-start = ((), (), s32[]{:S(2)}) async-start(), calls=%async_computation | async-start | bytes 2162688 | tf_op jit(solution)/shard_map/all_gather | solution.py:90
  7.3 120.7 %all-gather.7.cloned.1.call-start = ((), (), s32[]{:S(2)}) async-start(), calls=%async_computation.1 | async-start | bytes 2162688 | tf_op jit(solution)/shard_map/all_gather | solution.py:91
  8.0 165.2 %all-gather.9.cloned.1.call-start = ((), (), s32[]{:S(2)}) async-start(), calls=%async_computation.2 | async-start | bytes 1769472 | tf_op jit(solution)/shard_map/all_gather | solution.py:119
  9.8 5.7 %copy-start.10 = (s32[8]{0:T(128)S(1)}, s32[8]{0:T(128)}, u32[]{:S(2)}) copy-start(s32[8]{0:T(128)} %param.17) | copy-start | bytes 100
  9.8 5.8 %copy-start.11 = (s32[8]{0:T(128)S(1)}, s32[8]{0:T(128)}, u32[]{:S(2)}) copy-start(s32[8]{0:T(128)} %param.18) | copy-start | bytes 100
  9.9 208.4 %all-gather.11.cloned.1.call-start = ((), (), s32[]{:S(2)}) async-start(), calls=%async_computation.3 | async-start | bytes 1769472 | tf_op jit(solution)/shard_map/all_gather | solution.py:120
  131.1 2.3 copy-start.4
  135.8 1.3 copy-start.5
  140.2 2.3 copy-start.4
  144.9 1.3 copy-start.5
  149.3 2.3 copy-start.4
  154.0 1.3 copy-start.5
  158.4 2.3 copy-start.4
  163.1 1.3 copy-start.5
  222.2 2.2 copy-start.3
  222.2 2.3 copy-start
  222.3 3.8 %copy-start.6 = (f32[2,4,5,96]{3,2,1,0:T(8,128)S(1)}, f32[2,4,5,96]{3,2,1,0:T(8,128)}, u32[]{:S(2)}) copy-start(f32[2,4,5,96]{3,2,1,0:T(8,128)} %get-tuple-element.686) | copy-start | bytes 46084 | tf_op jit(solution)/shard_map/while
  226.1 2.0 copy-start.7
  232.6 2.2 copy-start.3
  232.6 2.3 copy-start
  232.6 3.8 %copy-start.6 = (f32[2,4,5,96]{3,2,1,0:T(8,128)S(1)}, f32[2,4,5,96]{3,2,1,0:T(8,128)}, u32[]{:S(2)}) copy-start(f32[2,4,5,96]{3,2,1,0:T(8,128)} %get-tuple-element.686) | copy-start | bytes 46084 | tf_op jit(solution)/shard_map/while
  236.5 2.0 copy-start.7
  243.0 2.2 copy-start.3
  243.0 2.3 copy-start
  243.0 3.8 %copy-start.6 = (f32[2,4,5,96]{3,2,1,0:T(8,128)S(1)}, f32[2,4,5,96]{3,2,1,0:T(8,128)}, u32[]{:S(2)}) copy-start(f32[2,4,5,96]{3,2,1,0:T(8,128)} %get-tuple-element.686) | copy-start | bytes 46084 | tf_op jit(solution)/shard_map/while
  246.8 2.0 copy-start.7
  251.7 31.0 %copy-start.9 = (s32[8]{0:T(128)S(1)}, s32[8]{0:T(128)}, u32[]{:S(2)}) copy-start(s32[8]{0:T(128)} %param.19) | copy-start | bytes 100
  254.4 13.8 %collective-permute-start = (bf16[2,96,2560]{2,1,0:T(8,128)(2,1)S(1)}, bf16[2,96,2560]{2,1,0:T(8,128)(2,1)S(1)}, u32[]{:S(2)}, u32[]{:S(2)}) collective-permute-start(bf16[2,96,2560]{2,1,0:T(8,128)(2,1)S(1)} %copy.47), channel_id=1, source_target_pairs={{0,8},{8,16},{16,24},{24,0},{1,9},{9,17},{17,25},{25,1},{2,10},{10... | collective-permute-start | bytes 2949128 | tf_op jit(solution)/shard_map/ppermute | solution.py:137
  268.2 0.9 copy-start.8
  269.1 13.6 %collective-permute-start.1 = (bf16[2,96,2560]{2,1,0:T(8,128)(2,1)S(1)}, bf16[2,96,2560]{2,1,0:T(8,128)(2,1)}, u32[]{:S(2)}, u32[]{:S(2)}) collective-permute-start(bf16[2,96,2560]{2,1,0:T(8,128)(2,1)S(1)} %collective-permute-done), channel_id=1, source_target_pairs={{0,8},{8,16},{16,24},{24,0},{1,9},{9,17},{17,25},{25,1},{2,10},{10... | collective-permute-start | bytes 2949128 | tf_op jit(solution)/shard_map/ppermute | solution.py:137
  282.7 13.8 %collective-permute-start.2 = (bf16[2,96,2560]{2,1,0:T(8,128)(2,1)}, bf16[2,96,2560]{2,1,0:T(8,128)(2,1)}, u32[]{:S(2)}, u32[]{:S(2)}) collective-permute-start(bf16[2,96,2560]{2,1,0:T(8,128)(2,1)} %collective-permute-done.1), channel_id=1, source_target_pairs={{0,8},{8,16},{16,24},{24,0},{1,9},{9,17},{17,25},{25,1},{2,10},{10... | collective-permute-start | bytes 2949128 | tf_op jit(solution)/shard_map/ppermute | solution.py:137
  300.4 2.0 copy-start.2
  302.0 1.3 copy-start.1
Sparse Core Ops, SparseCore 0:
  10.3 59.2 all-gather.4
  72.6 55.3 all-gather.6
  130.2 43.0 all-gather.8
  175.3 42.9 all-gather.10
